TPU v7x, 256 devices: a whole 4x4x8 slice. The times are simulated.
256 devices in a mesh: track: 16 (over z, x_lo), tm: 16 (over x_hi, y, core).
Axes of the slice: x: 4 (x_hi: 2, x_lo: 2; x = x_hi * 2 + x_lo), y: 4, z: 8, core: 2. Of those that a mesh axis runs over, the one named last changes fastest.
Arguments:
- positions: float32 [3, 32, 6144], P(None, 'tm', 'track'), may hold values from -6 to 6
- embeddings: float32 [32, 128, 6144], P('tm', None, 'track'), may hold values from -6 to 6
- visible: int32 [32, 6144], P('tm', 'track'), may hold values 0 or 1
Outputs:
- grad_positions: float32 [3, 32, 6144], P(None, 'tm', 'track')
- grad_embeddings: float32 [32, 128, 6144], P('tm', None, 'track')
- mean_loss: float32 [], replicated
All inputs are finite; a program needn't handle non-finite values. No bound on the sum of `visible` on one device may be relied on, other than what follows from the above.
Results may differ from a plain program's by a relative error of at most 0.00014.
Values sent between devices are 32-bit elements; how exact they have to be, the bound alone decides.
A program may use at most 128 MiB of HBM per device.

v0:
```python
import math
import jax
import jax.numpy as jnp
from jax import lax
from jax.sharding import PartitionSpec as P

rigidity = 4.0
highest = lax.Precision.HIGHEST


def shifted(array, axis, by):
    size = lax.axis_size(axis)
    pairs = [(i, i + by) for i in range(size) if 0 <= i + by < size]
    return lax.ppermute(array, axis, pairs)


def tile_terms(pos_a, mask_a, emb_a, pos_b, mask_b, emb_b, weight_scale):
    inv_root = 1.0 / math.sqrt(emb_a.shape[1])
    offset = pos_a[:, :, :, None] - pos_b[:, :, None, :]
    distance = jnp.sqrt(jnp.sum(offset * offset, axis=0) + 1.0)
    change = distance[1:] - distance[:-1]
    both_seen = mask_a[:, :, None] * mask_b[:, None, :]
    seen_pair = both_seen[1:] * both_seen[:-1]
    logits = jnp.einsum("fei,fej->fij", emb_a, emb_b, precision=highest) * inv_root
    affinity = jax.nn.sigmoid(logits)
    squared = seen_pair * change * change
    energy = jnp.sum(affinity * squared)
    grad_change = 2.0 * weight_scale * affinity * seen_pair * change
    padding = jnp.zeros_like(grad_change[:1])
    grad_dist = jnp.concatenate([padding, grad_change], 0) - jnp.concatenate(
        [grad_change, padding], 0
    )
    scaled = (grad_dist / distance)[None] * offset
    grad_pos_a = jnp.sum(scaled, axis=3)
    grad_pos_b = -jnp.sum(scaled, axis=2)
    grad_logit = weight_scale * squared * affinity * (1.0 - affinity) * inv_root
    grad_emb_a = jnp.einsum("fij,fej->fei", grad_logit, emb_b, precision=highest)
    grad_emb_b = jnp.einsum("fij,fei->fej", grad_logit, emb_a, precision=highest)
    return (energy, grad_pos_a, grad_emb_a, grad_pos_b, grad_emb_b)


def on_device(positions, embeddings, visible):
    frames_local = embeddings.shape[0]
    block_width = embeddings.shape[2]
    tracks = block_width * lax.axis_size("track")
    frames = frames_local * lax.axis_size("tm")
    weight_scale = rigidity / math.sqrt(tracks)
    seen_mask = visible.astype(jnp.float32)
    next_pos, next_mask = shifted((positions[:, :1], seen_mask[:1]), "tm", -1)
    pos_ext = jnp.concatenate([positions, next_pos], 1)
    mask_ext = jnp.concatenate([seen_mask, next_mask], 0)
    packed = jnp.concatenate([pos_ext, mask_ext[None]], 0)

    def own_tile(others_packed, others_emb):
        return tile_terms(
            pos_ext,
            mask_ext,
            embeddings,
            others_packed[:3],
            others_packed[3],
            others_emb,
            weight_scale,
        )

    initial = (jnp.zeros_like(pos_ext), jnp.zeros_like(embeddings), jnp.zeros((), jnp.float32))
    piece_packed = lax.all_gather(packed, "track", axis=2, tiled=True)
    piece_emb = lax.all_gather(embeddings, "track", axis=2, tiled=True)
    columns = piece_emb.shape[2]
    blocks = columns // block_width
    split_packed = jnp.moveaxis(
        piece_packed.reshape(4, frames_local + 1, blocks, block_width), 2, 0
    )
    split_emb = jnp.moveaxis(
        piece_emb.reshape(frames_local, piece_emb.shape[1], blocks, block_width), 2, 0
    )

    def advance(inner, others):
        energy, grad_pos_a, grad_emb_a, unused_pos, unused_emb = own_tile(others[0], others[1])
        return ((inner[0] + grad_pos_a, inner[1] + grad_emb_a, inner[2] + energy), None)

    result, unused = lax.scan(advance, initial, (split_packed, split_emb))
    grad_pos, grad_emb, energy_sum = result
    energy_sum = 0.5 * energy_sum
    incoming = shifted(grad_pos[:, -1:], "tm", 1)
    grad_positions = grad_pos[:, :-1]
    grad_positions = jnp.concatenate([grad_positions[:, :1] + incoming, grad_positions[:, 1:]], 1)
    total = lax.psum(energy_sum, ("track", "tm"))
    mean_loss = total / (tracks * (tracks - 1) / 2.0 * (frames - 1))
    return (grad_positions, grad_emb, mean_loss)


def solution(mesh):
    in_specs = (P(None, "tm", "track"), P("tm", None, "track"), P("tm", "track"))
    out_specs = (P(None, "tm", "track"), P("tm", None, "track"), P())
    return jax.shard_map(
        on_device, mesh=mesh, in_specs=in_specs, out_specs=out_specs, check_vma=False
    )
```

profile of v0, /device:TPU:1, one launch (start us, length us, event | category | flops | bytes accessed | tf_op | source)
XLA Modules:
  0.0 581.3 jit_solution(791380038999158030)
XLA Ops:
  7.2 1.9 copy.30
  9.9 5.1 collective-permute-start
  15.7 1.9 collective-permute-start.1
  17.6 3.0 collective-permute-done.1
  21.3 41.1 %all_gather.7 = f32[4,3,6144]{2,1,0:T(4,128)S(1)} all-gather(f32[4,3,384]{2,1,0:T(4,128)S(1)} %pad_maximum_fusion), channel_id=1, replica_groups=mesh['track'=16,'tm'=16] {'track'}, dimensions={2}, use_global_device_ids=true | all-gather | bytes 313344 | tf_op jit(solution)/shard_map/all_gather | solution.py:66
  63.9 97.0 %all-gather.2.cloned.1.call-done = f32[2,128,6144]{1,2,0:T(8,128)} async-done(((f32[2,128,384]{1,2,0:T(8,128)}), f32[2,128,6144]{1,2,0:T(8,128)}) %all-gather.2.cloned.1.call-update) | async-done | bytes 6291472 | tf_op jit(solution)/shard_map/all_gather | solution.py:67
  160.9 327.7 %while.15 = (s32[]{:T(128)}, f32[3,3,384]{2,1,0:T(4,128)}, f32[2,128,384]{2,1,0:T(8,128)}, f32[]{:T(128)}, f32[16,2,128,384]{2,3,0,1:T(8,128)}, /*index=5*/f32[2...) while((s32[]{:T(128)}, f32[3,3,384]{2,1,0:T(4,128)}, ...), condition=%wide.region_4.5_spmd.clone, body=%wide.region_0.4_spmd.clone.sunk | while | flops 922389888 | bytes 49315164 | solution.py:81
  167.0 5.0 multiply_reduce_fusion.2
  172.7 4.3 convolution_add_fusion.2
  187.4 5.0 multiply_reduce_fusion.2
  193.2 4.4 convolution_add_fusion.2
  207.9 5.0 multiply_reduce_fusion.2
  213.6 4.4 convolution_add_fusion.2
  219.9 1.8 fusion.35
  228.4 5.0 multiply_reduce_fusion.2
  234.1 4.4 convolution_add_fusion.2
  248.9 5.0 multiply_reduce_fusion.2
  254.6 4.4 convolution_add_fusion.2
  260.9 1.8 fusion.35
  269.4 5.0 multiply_reduce_fusion.2
  275.1 4.4 convolution_add_fusion.2
  281.3 1.8 fusion.35
  289.9 5.0 multiply_reduce_fusion.2
  295.6 4.4 convolution_add_fusion.2
  310.3 5.0 multiply_reduce_fusion.2
  316.1 4.4 convolution_add_fusion.2
  322.3 1.8 fusion.35
  330.8 5.0 multiply_reduce_fusion.2
  336.6 4.4 convolution_add_fusion.2
  351.3 5.0 multiply_reduce_fusion.2
  357.1 4.4 convolution_add_fusion.2
  363.3 1.8 fusion.35
  371.8 5.0 multiply_reduce_fusion.2
  377.5 4.4 convolution_add_fusion.2
  383.8 1.8 fusion.35
  392.3 5.0 multiply_reduce_fusion.2
  398.0 4.4 convolution_add_fusion.2
  404.3 1.8 fusion.35
  412.8 5.0 multiply_reduce_fusion.2
  418.5 4.4 convolution_add_fusion.2
  433.3 5.0 multiply_reduce_fusion.2
  439.0 4.4 convolution_add_fusion.2
  453.7 5.0 multiply_reduce_fusion.2
  459.5 4.4 convolution_add_fusion.2
  474.2 5.0 multiply_reduce_fusion.2
  480.0 4.4 convolution_add_fusion.2
  489.4 4.8 collective-permute-start.2
  494.2 77.0 %psum.7 = f32[]{:T(128)} all-reduce(f32[]{:T(128)S(6)} %mul_shard_map.3), channel_id=1, replica_groups=mesh['track'=16,'tm'=16] {'track','tm'}, use_global_device_ids=true, to_apply=%region_5.6 | all-reduce | flops 1 | bytes 8 | tf_op jit(solution)/shard_map/psum | solution.py:87
  (379 shorter events, 157.2 us)
Async XLA Ops:
  7.2 56.1 %copy-start.6 = (f32[3,2,384]{2,1,0:T(2,128)S(1)}, f32[3,2,384]{2,1,0:T(2,128)}, u32[]{:S(2)}) copy-start(f32[3,2,384]{2,1,0:T(2,128)} %param.5) | copy-start | bytes 27652
  7.2 153.8 %all-gather.2.cloned.1.call-start = ((), (), s32[]{:S(2)}) async-start(), calls=%async_computation | async-start | bytes 6684672 | tf_op jit(solution)/shard_map/all_gather | solution.py:67
  9.9 7.7 %collective-permute-start = (f32[1,384]{1,0:T(1,128)S(1)}, f32[1,384]{1,0:T(1,128)S(1)}, u32[]{:S(2)}, u32[]{:S(2)}) collective-permute-start(f32[1,384]{1,0:T(1,128)S(1)} %slice.53), channel_id=1, source_target_pairs={{1,0},{2,1},{3,2},{4,3},{5,4},{6,5},{7,6},{8,7},{9,8},{10,9},{11,1... | collective-permute-start | bytes 4616 | tf_op jit(solution)/shard_map/ppermute | solution.py:14
  15.7 4.9 collective-permute-start.1
  166.7 5.4 copy-start
  172.7 4.3 copy-start.1
  178.9 1.8 copy-start.3
  187.1 5.4 copy-start
  193.1 4.4 copy-start.1
  207.6 5.4 copy-start
  213.6 4.4 copy-start.1
  219.9 1.8 copy-start.3
  228.0 5.4 copy-start
  234.1 4.4 copy-start.1
  248.5 5.4 copy-start
  254.6 4.4 copy-start.1
  260.8 1.8 copy-start.3
  269.0 5.4 copy-start
  275.1 4.4 copy-start.1
  281.3 1.8 copy-start.3
  289.5 5.4 copy-start
  295.6 4.4 copy-start.1
  301.8 1.8 copy-start.3
  310.0 5.4 copy-start
  316.1 4.4 copy-start.1
  322.3 1.8 copy-start.3
  330.5 5.4 copy-start
  336.6 4.4 copy-start.1
  342.8 1.8 copy-start.3
  351.0 5.4 copy-start
  357.0 4.4 copy-start.1
  363.3 1.8 copy-start.3
  371.4 5.4 copy-start
  377.5 4.4 copy-start.1
  383.8 1.8 copy-start.3
  391.9 5.4 copy-start
  398.0 4.4 copy-start.1
  404.3 1.8 copy-start.3
  412.4 5.4 copy-start
  418.5 4.4 copy-start.1
  432.9 5.4 copy-start
  439.0 4.4 copy-start.1
  445.2 1.8 copy-start.3
  453.4 5.4 copy-start
  459.5 4.4 copy-start.1
  473.9 5.4 copy-start
  480.0 4.4 copy-start.1
  489.4 82.5 %collective-permute-start.2 = (f32[3,1,384]{2,1,0:T(1,128)S(1)}, f32[3,1,384]{2,1,0:T(1,128)S(1)}, u32[]{:S(2)}, u32[]{:S(2)}) collective-permute-start(f32[3,1,384]{2,1,0:T(1,128)S(1)} %slice.41), channel_id=1, source_target_pairs={{0,1},{1,2},{2,3},{3,4},{4,5},{5,6},{6,7},{7,8},{8,9},{9,10},{10,1... | collective-permute-start | bytes 13832 | tf_op jit(solution)/shard_map/ppermute | solution.py:14
  (53 other events, 44.3 us)
Sparse Core Ops, SparseCore 0:
  9.8 151.1 all-gather.1
where the time goes:
time: 586 us; the launch traced here: 581 us
  matrix products  151 us (26%)
  blocking collectives  118 us (20%)
  waiting for transfers between devices  100 us (17%)
  local copies, waits for them, and re-layouts  94.3 us (16%)
  other arithmetic  77.4 us (13%)
  between operations  15.9 us (3%)
  loops' own time  12.7 us (2%)
  starting transfers between devices  11.9 us (2%)
    all_gather x1, waiting for transfers between devices, on_device(): piece_emb = lax.all_gather(embeddings, 'track', axis=2, tiled=True)  97 us
    dot_general x16, matrix products, tile_terms(): jnp.einsum('fei,fej->fij', emb_a, emb_b, precision=highest) * inv_root  80.6 us
    psum x1, blocking collectives, on_device(): total = lax.psum(energy_sum, ('track', 'tm'))  77 us
    dot_general x16, matrix products, tile_terms(): jnp.einsum('fij,fej->fei', grad_logit, emb_b, precision=highest)  70.5 us
    all_gather x1, blocking collectives, on_device(): piece_packed = lax.all_gather(packed, 'track', axis=2, tiled=True)  41.1 us
    reduce_sum x16, other arithmetic, tile_terms(): grad_pos_a = jnp.sum(scaled, axis=3)  28.8 us
    while x224, local copies, waits for them, and re-layouts  24.9 us
    reduce_sum x16, other arithmetic, tile_terms(): distance = jnp.sqrt(jnp.sum(offset * offset, axis=0) + 1.0)  24.9 us
  transfers between devices with their start and end apart: 4, of which 2 were waited for; matrix products, arithmetic and copies ran while one was open for 1% of the time, Pallas kernels for 0%

commit v1 on v0

--- a/solution.py
+++ b/solution.py
@@ -84,7 +84,7 @@
     incoming = shifted(grad_pos[:, -1:], "tm", 1)
     grad_positions = grad_pos[:, :-1]
     grad_positions = jnp.concatenate([grad_positions[:, :1] + incoming, grad_positions[:, 1:]], 1)
-    total = lax.psum(energy_sum, ("track", "tm"))
+    total = lax.psum(lax.psum(energy_sum, "track"), "tm")
     mean_loss = total / (tracks * (tracks - 1) / 2.0 * (frames - 1))
     return (grad_positions, grad_emb, mean_loss)
 

time: 586 us -> 572 us (0.976)
  blocking collectives: 118 us -> 106 us
    psum x1 -> x2, blocking collectives: 77 us -> 65.2 us  [on_device(): total = lax.psum(lax.psum(energy_sum, 'track'), 'tm')]
where the time goes in v1:
time: 572 us; the launch traced here: 567 us
  matrix products  150 us (26%)
  blocking collectives  106 us (19%)
  waiting for transfers between devices  101 us (18%)
  local copies, waits for them, and re-layouts  94.2 us (16%)
  other arithmetic  77.4 us (14%)
  between operations  15.9 us (3%)
  starting transfers between devices  11.4 us (2%)
  loops' own time  10.9 us (2%)
    all_gather x1, waiting for transfers between devices, on_device(): piece_emb = lax.all_gather(embeddings, 'track', axis=2, tiled=True)  98.2 us
    dot_general x16, matrix products, tile_terms(): jnp.einsum('fei,fej->fij', emb_a, emb_b, precision=highest) * inv_root  79.7 us
    dot_general x16, matrix products, tile_terms(): jnp.einsum('fij,fej->fei', grad_logit, emb_b, precision=highest)  70.5 us
    psum x2, blocking collectives, on_device(): total = lax.psum(lax.psum(energy_sum, 'track'), 'tm')  65.2 us
    all_gather x1, blocking collectives, on_device(): piece_packed = lax.all_gather(packed, 'track', axis=2, tiled=True)  40.4 us
    reduce_sum x16, other arithmetic, tile_terms(): grad_pos_a = jnp.sum(scaled, axis=3)  28.8 us
    reduce_sum x16, other arithmetic, tile_terms(): distance = jnp.sqrt(jnp.sum(offset * offset, axis=0) + 1.0)  24.9 us
    while x224, local copies, waits for them, and re-layouts  24.9 us
  transfers between devices with their start and end apart: 4, of which 2 were waited for; matrix products, arithmetic and copies ran while one was open for 1% of the time, Pallas kernels for 0%

profile of v1, /device:TPU:1, one launch (start us, length us, event | category | flops | bytes accessed | tf_op | source)
XLA Modules:
  0.0 566.7 jit_solution(10009080141768730305)
XLA Ops:
  7.2 1.9 copy.30
  9.8 5.1 collective-permute-start
  15.7 1.9 collective-permute-start.1
  17.6 3.0 collective-permute-done.1
  21.3 40.4 %all_gather.7 = f32[4,3,6144]{2,1,0:T(4,128)S(1)} all-gather(f32[4,3,384]{2,1,0:T(4,128)S(1)} %pad_maximum_fusion), channel_id=1, replica_groups=mesh['track'=16,'tm'=16] {'track'}, dimensions={2}, use_global_device_ids=true | all-gather | bytes 313344 | tf_op jit(solution)/shard_map/all_gather | solution.py:66
  63.3 98.2 %all-gather.2.cloned.1.call-done = f32[2,128,6144]{1,2,0:T(8,128)} async-done(((f32[2,128,384]{1,2,0:T(8,128)}), f32[2,128,6144]{1,2,0:T(8,128)}) %all-gather.2.cloned.1.call-update) | async-done | bytes 6291472 | tf_op jit(solution)/shard_map/all_gather | solution.py:67
  161.5 324.9 %while.15 = (s32[]{:T(128)}, f32[3,3,384]{2,1,0:T(4,128)}, f32[2,128,384]{2,1,0:T(8,128)}, f32[]{:T(128)}, f32[16,2,128,384]{2,3,0,1:T(8,128)}, /*index=5*/f32[2...) while((s32[]{:T(128)}, f32[3,3,384]{2,1,0:T(4,128)}, ...), condition=%wide.region_4.5_spmd.clone, body=%wide.region_0.4_spmd.clone.sunk | while | flops 922389888 | bytes 49315164 | solution.py:81
  167.5 5.0 multiply_reduce_fusion.2
  173.1 4.3 convolution_add_fusion.2
  187.8 5.0 multiply_reduce_fusion.2
  193.3 4.4 convolution_add_fusion.2
  199.6 1.8 fusion.35
  208.1 5.0 multiply_reduce_fusion.2
  213.6 4.4 convolution_add_fusion.2
  219.9 1.8 fusion.35
  228.4 5.0 multiply_reduce_fusion.2
  233.9 4.4 convolution_add_fusion.2
  240.2 1.8 fusion.35
  248.7 5.0 multiply_reduce_fusion.2
  254.3 4.4 convolution_add_fusion.2
  260.5 1.8 fusion.35
  269.0 5.0 multiply_reduce_fusion.2
  274.6 4.4 convolution_add_fusion.2
  280.8 1.8 fusion.35
  289.3 5.0 multiply_reduce_fusion.2
  294.9 4.4 convolution_add_fusion.2
  301.1 1.8 fusion.35
  309.6 5.0 multiply_reduce_fusion.2
  315.2 4.4 convolution_add_fusion.2
  329.9 5.0 multiply_reduce_fusion.2
  335.5 4.4 convolution_add_fusion.2
  350.3 5.0 multiply_reduce_fusion.2
  355.8 4.4 convolution_add_fusion.2
  370.6 5.0 multiply_reduce_fusion.2
  376.1 4.4 convolution_add_fusion.2
  390.9 5.0 multiply_reduce_fusion.2
  396.4 4.4 convolution_add_fusion.2
  411.2 5.0 multiply_reduce_fusion.2
  416.8 4.4 convolution_add_fusion.2
  431.5 5.0 multiply_reduce_fusion.2
  437.1 4.4 convolution_add_fusion.2
  451.8 5.0 multiply_reduce_fusion.2
  457.4 4.4 convolution_add_fusion.2
  472.1 5.0 multiply_reduce_fusion.2
  477.7 4.4 convolution_add_fusion.2
  487.1 4.3 collective-permute-start.2
  491.4 26.6 %psum.14 = f32[]{:T(128)} all-reduce(f32[]{:T(128)S(6)} %mul_shard_map.3), channel_id=1, replica_groups=mesh['track'=16,'tm'=16] {'track'}, use_global_device_ids=true, to_apply=%region_5.6 | all-reduce | flops 1 | bytes 8 | tf_op jit(solution)/shard_map/psum | solution.py:87
  518.1 38.5 %psum.15 = f32[]{:T(128)} all-reduce(f32[]{:T(128)} %psum.14), channel_id=1, replica_groups=mesh['track'=16,'tm'=16] {'tm'}, use_global_device_ids=true, to_apply=%region_6.7 | all-reduce | flops 1 | bytes 8 | tf_op jit(solution)/shard_map/psum | solution.py:87
  (380 shorter events, 158.9 us)
Async XLA Ops:
  7.2 55.5 %copy-start.6 = (f32[3,2,384]{2,1,0:T(2,128)S(1)}, f32[3,2,384]{2,1,0:T(2,128)}, u32[]{:S(2)}) copy-start(f32[3,2,384]{2,1,0:T(2,128)} %param.5) | copy-start | bytes 27652
  7.2 154.3 %all-gather.2.cloned.1.call-start = ((), (), s32[]{:S(2)}) async-start(), calls=%async_computation | async-start | bytes 6684672 | tf_op jit(solution)/shard_map/all_gather | solution.py:67
  9.8 7.7 %collective-permute-start = (f32[1,384]{1,0:T(1,128)S(1)}, f32[1,384]{1,0:T(1,128)S(1)}, u32[]{:S(2)}, u32[]{:S(2)}) collective-permute-start(f32[1,384]{1,0:T(1,128)S(1)} %slice.53), channel_id=1, source_target_pairs={{1,0},{2,1},{3,2},{4,3},{5,4},{6,5},{7,6},{8,7},{9,8},{10,9},{11,1... | collective-permute-start | bytes 4616 | tf_op jit(solution)/shard_map/ppermute | solution.py:14
  15.7 4.9 collective-permute-start.1
  167.2 5.3 copy-start
  173.1 4.3 copy-start.1
  187.4 5.3 copy-start
  193.3 4.4 copy-start.1
  199.6 1.8 copy-start.3
  207.7 5.3 copy-start
  213.6 4.4 copy-start.1
  219.9 1.8 copy-start.3
  228.0 5.3 copy-start
  233.9 4.4 copy-start.1
  240.2 1.8 copy-start.3
  248.3 5.3 copy-start
  254.3 4.4 copy-start.1
  260.5 1.8 copy-start.3
  268.7 5.3 copy-start
  274.6 4.4 copy-start.1
  280.8 1.8 copy-start.3
  289.0 5.3 copy-start
  294.9 4.4 copy-start.1
  301.1 1.8 copy-start.3
  309.3 5.3 copy-start
  315.2 4.4 copy-start.1
  321.4 1.8 copy-start.3
  329.6 5.3 copy-start
  335.5 4.4 copy-start.1
  341.7 1.8 copy-start.3
  349.9 5.3 copy-start
  355.8 4.4 copy-start.1
  362.1 1.8 copy-start.3
  370.2 5.3 copy-start
  376.1 4.4 copy-start.1
  382.4 1.8 copy-start.3
  390.5 5.3 copy-start
  396.4 4.4 copy-start.1
  402.7 1.8 copy-start.3
  410.8 5.3 copy-start
  416.7 4.4 copy-start.1
  431.1 5.3 copy-start
  437.1 4.4 copy-start.1
  451.5 5.3 copy-start
  457.4 4.4 copy-start.1
  471.8 5.3 copy-start
  477.7 4.4 copy-start.1
  487.1 70.2 %collective-permute-start.2 = (f32[3,1,384]{2,1,0:T(1,128)S(1)}, f32[3,1,384]{2,1,0:T(1,128)S(1)}, u32[]{:S(2)}, u32[]{:S(2)}) collective-permute-start(f32[3,1,384]{2,1,0:T(1,128)S(1)} %slice.41), channel_id=1, source_target_pairs={{0,1},{1,2},{2,3},{3,4},{4,5},{5,6},{6,7},{7,8},{8,9},{9,10},{10,1... | collective-permute-start | bytes 13832 | tf_op jit(solution)/shard_map/ppermute | solution.py:14
  (53 other events, 44.2 us)
Sparse Core Ops, SparseCore 0:
  9.8 151.6 all-gather.1
